TPU v7x, 32 devices: a whole 2x2x4 slice. The times are simulated.
32 devices in a mesh: tenant: 8 (over z, core), row: 4 (over y, x).
Axes of the slice: x: 2, y: 2, z: 4, core: 2. Of those that a mesh axis runs over, the one named last changes fastest.
Arguments:
- b_factors: float32 [64, 16, 8192], P('tenant', None, 'row'), may hold values from -6 to 6
- a_factors: float32 [64, 16, 8192], P('tenant', None, 'row'), may hold values from -6 to 6
- u_start: float32 [8192, 256], P('row'), may hold values from -0.0625 to 0.0625
- v_start: float32 [8192, 256], P('row'), may hold values from -0.0625 to 0.0625
Outputs:
- u_scaled: float32 [8192, 256], P('row')
- v_scaled: float32 [8192, 256], P('row')
- core_left: float32 [64, 16, 256], P('tenant')
- core_right: float32 [64, 16, 256], P('tenant')
All inputs are finite; a program needn't handle non-finite values.
Results may differ from a plain program's by a relative error of at most 0.0003.
Values sent between devices are 32-bit elements; how exact they have to be, the bound alone decides.
A program may use at most 64 MiB of HBM per device.

v0:
```python
import math

import jax
import jax.numpy as jnp
from jax import lax
from jax.sharding import PartitionSpec as P

D = 8192


HIGH = lax.Precision.HIGHEST


def project(factors, basis):
    return jnp.einsum("trd,dk->trk", factors, basis, precision=HIGH)


def normalize(matrix, gram):
    lower = jnp.linalg.cholesky(gram)
    return lax.linalg.triangular_solve(lower, matrix, left_side=False, lower=True, transpose_a=True)


def refresh(loading, coeffs):
    local_sum = jnp.einsum("trd,trk->dk", loading, coeffs, precision=HIGH)
    total = lax.psum(local_sum, "tenant")
    gram = lax.psum(jnp.dot(total.T, total, precision=HIGH), "row")
    return normalize(total, gram)


def local(b_factors, a_factors, u_start, v_start):
    left, right = lax.psum((project(b_factors, u_start), project(a_factors, v_start)), "row")
    weight = jnp.einsum("trk,tsk->trs", right, right, precision=HIGH)
    coeffs = jnp.einsum("trs,tsk->trk", weight, left, precision=HIGH)
    basis_u = refresh(b_factors, coeffs)
    left = lax.psum(project(b_factors, basis_u), "row")
    weight = jnp.einsum("trk,tsk->trs", left, left, precision=HIGH)
    coeffs = jnp.einsum("trs,tsk->trk", weight, right, precision=HIGH)
    basis_v = refresh(a_factors, coeffs)
    right = lax.psum(project(a_factors, basis_v), "row")
    scale = math.sqrt(D)
    return (basis_u * scale, basis_v * scale, left, right)


def solution(mesh):
    in_specs = (P("tenant", None, "row"), P("tenant", None, "row"), P("row", None), P("row", None))
    out_specs = (P("row", None), P("row", None), P("tenant", None, None), P("tenant", None, None))
    return jax.shard_map(local, mesh=mesh, in_specs=in_specs, out_specs=out_specs, check_vma=False)
```

profile of v0, /device:TPU:0, one launch (start us, length us, event | category | flops | bytes accessed | tf_op | source)
XLA Modules:
  0.0 532.5 jit_solution(5494314746530487109)
XLA Ops:
  8.8 3.2 fusion.4
  13.8 45.9 %all-reduce.22.cloned.1.call-done = (f32[8,16,256]{2,1,0:T(8,128)}, f32[8,16,256]{2,1,0:T(8,128)}) async-done(((f32[8,16,256]{2,1,0:T(8,128)}, f32[8,16,256]{2,1,0:T(8,128)}), (f32[8,16,256]{2,1,0:T(8,128)}, f32[8,16,256]{2,1,0:T(8,128)})) %all-reduce.22.cloned.1.call-update) | async-done | bytes 262160 | tf_op jit(solution)/shard_map/psum | solution.py:31
  62.1 3.2 convolution_bitcast_fusion.1
  65.4 65.2 %all-reduce.10.cloned.1.call-done = f32[2048,256]{0,1:T(8,128)} async-done(((f32[2048,256]{0,1:T(8,128)}), f32[2048,256]{0,1:T(8,128)}) %all-reduce.10.cloned.1.call-update) | async-done | bytes 2097168 | tf_op jit(solution)/shard_map/psum | solution.py:25
  130.6 4.8 fusion.38
  135.7 42.5 %all-reduce.12.cloned.1.call-done = f32[256,256]{0,1:T(8,128)} async-done(((f32[256,256]{0,1:T(8,128)}), f32[256,256]{0,1:T(8,128)}) %all-reduce.12.cloned.1.call-update) | async-done | bytes 262160 | tf_op jit(solution)/shard_map/psum | solution.py:26
  180.3 11.7 %cholesky.130 = f32[128,128]{1,0:T(8,128)S(1)} custom-call(f32[128,128]{1,0:T(8,128)S(1)} %cholesky.194), custom_call_target="Cholesky" | custom-call | tf_op jit(solution)/shard_map/jit(cholesky)/cholesky | solution.py:19
  192.0 9.8 %custom-call.13 = f32[1,128,128]{1,2,0:T(8,128)S(1)} custom-call(f32[1,128,128]{2,1,0:T(8,128)S(1)} %get-tuple-element.55), custom_call_target="InvertDiagBlocksLowerTriangular" | custom-call | tf_op jit(solution)/shard_map/jit(cholesky)/cholesky | solution.py:19
  202.4 11.7 %cholesky.147 = f32[128,128]{1,0:T(8,128)S(1)} custom-call(f32[128,128]{1,0:T(8,128)S(1)} %convolution_subtract_fusion.3), custom_call_target="Cholesky" | custom-call | tf_op jit(solution)/shard_map/jit(cholesky)/cholesky | solution.py:19
  216.2 4.4 while.4
  220.6 19.7 %custom-call.14 = f32[2,128,128]{1,2,0:T(8,128)S(1)} custom-call(f32[2,128,128]{2,1,0:T(8,128)S(1)} %get-tuple-element.20), custom_call_target="InvertDiagBlocksLowerTriangular" | custom-call | tf_op jit(solution)/shard_map/triangular_solve/custom-call.0 | solution.py:20
  248.8 42.3 %all-reduce.14.cloned.1.call-done = f32[8,16,256]{2,1,0:T(8,128)} async-done(((f32[8,16,256]{2,1,0:T(8,128)}), f32[8,16,256]{2,1,0:T(8,128)}) %all-reduce.14.cloned.1.call-update) | async-done | bytes 131088 | tf_op jit(solution)/shard_map/psum | solution.py:35
  292.6 4.4 convolution_bitcast_fusion
  297.1 65.2 %all-reduce.16.cloned.1.call-done = f32[2048,256]{0,1:T(8,128)} async-done(((f32[2048,256]{0,1:T(8,128)}), f32[2048,256]{0,1:T(8,128)}) %all-reduce.16.cloned.1.call-update) | async-done | bytes 2097168 | tf_op jit(solution)/shard_map/psum | solution.py:25
  362.2 4.8 fusion.41
  369.9 3.0 copy.14
  373.0 36.9 %all-reduce.18.cloned.1.call-done = f32[256,256]{0,1:T(8,128)} async-done(((f32[256,256]{0,1:T(8,128)}), f32[256,256]{0,1:T(8,128)}) %all-reduce.18.cloned.1.call-update) | async-done | bytes 262160 | tf_op jit(solution)/shard_map/psum | solution.py:26
  412.0 11.7 %cholesky.164 = f32[128,128]{1,0:T(8,128)S(1)} custom-call(f32[128,128]{1,0:T(8,128)S(1)} %cholesky.197), custom_call_target="Cholesky" | custom-call | tf_op jit(solution)/shard_map/jit(cholesky)/cholesky | solution.py:19
  424.3 9.8 %custom-call.15 = f32[1,128,128]{1,2,0:T(8,128)S(1)} custom-call(f32[1,128,128]{2,1,0:T(8,128)S(1)} %get-tuple-element.51), custom_call_target="InvertDiagBlocksLowerTriangular" | custom-call | tf_op jit(solution)/shard_map/jit(cholesky)/cholesky | solution.py:19
  434.7 11.7 %cholesky.181 = f32[128,128]{1,0:T(8,128)S(1)} custom-call(f32[128,128]{1,0:T(8,128)S(1)} %convolution_subtract_fusion.2), custom_call_target="Cholesky" | custom-call | tf_op jit(solution)/shard_map/jit(cholesky)/cholesky | solution.py:19
  448.4 4.0 while.5
  452.4 19.9 %custom-call.16 = f32[2,128,128]{1,2,0:T(8,128)S(1)} custom-call(f32[2,128,128]{2,1,0:T(8,128)S(1)} %get-tuple-element.21), custom_call_target="InvertDiagBlocksLowerTriangular" | custom-call | tf_op jit(solution)/shard_map/triangular_solve/custom-call.0 | solution.py:20
  483.6 2.9 copy.15
  486.6 36.6 %all-reduce.20.cloned.1.call-done = f32[8,16,256]{2,1,0:T(8,128)} async-done(((f32[8,16,256]{2,1,0:T(8,128)}), f32[8,16,256]{2,1,0:T(8,128)}) %all-reduce.20.cloned.1.call-update) | async-done | bytes 131088 | tf_op jit(solution)/shard_map/psum | solution.py:39
  (92 shorter events, 47.8 us)
Async XLA Ops:
  7.2 1.6 copy-start
  7.2 52.5 %all-reduce.22.cloned.1.call-start = ((), (), s32[]{:S(2)}) async-start(), calls=%async_computation.6 | async-start | bytes 524288 | tf_op jit(solution)/shard_map/psum | solution.py:31
  8.8 3.2 copy-start.7
  8.8 3.2 copy-start.9
  11.9 50.2 %copy-start.5 = (f32[8,16,2048]{2,1,0:T(8,128)S(1)}, f32[8,16,2048]{2,1,0:T(8,128)}, u32[]{:S(2)}) copy-start(f32[8,16,2048]{2,1,0:T(8,128)} %param.7) | copy-start | bytes 3145732
  13.7 116.8 %all-reduce.10.cloned.1.call-start = ((), (), s32[]{:S(2)}) async-start(), calls=%async_computation | async-start | bytes 4194304 | tf_op jit(solution)/shard_map/psum | solution.py:25
  65.3 112.9 %all-reduce.12.cloned.1.call-start = ((), (), s32[]{:S(2)}) async-start(), calls=%async_computation.1 | async-start | bytes 524288 | tf_op jit(solution)/shard_map/psum | solution.py:26
  135.4 155.7 %all-reduce.14.cloned.1.call-start = ((), (), s32[]{:S(2)}) async-start(), calls=%async_computation.2 | async-start | bytes 262144 | tf_op jit(solution)/shard_map/psum | solution.py:35
  240.3 2.4 copy-start.1
  242.7 3.1 copy-start.6
  244.9 1.0 copy-start.3
  245.8 46.5 %copy-start.10 = (f32[8,16,256]{2,1,0:T(8,128)S(1)}, f32[8,16,256]{2,1,0:T(8,128)}, u32[]{:S(2)}) copy-start(f32[8,16,256]{2,1,0:T(8,128)} %get-tuple-element.42) | copy-start | bytes 393220
  248.7 113.5 %all-reduce.16.cloned.1.call-start = ((), (), s32[]{:S(2)}) async-start(), calls=%async_computation.3 | async-start | bytes 4194304 | tf_op jit(solution)/shard_map/psum | solution.py:25
  297.0 112.8 %all-reduce.18.cloned.1.call-start = ((), (), s32[]{:S(2)}) async-start(), calls=%async_computation.4 | async-start | bytes 524288 | tf_op jit(solution)/shard_map/psum | solution.py:26
  367.1 156.1 %all-reduce.20.cloned.1.call-start = ((), (), s32[]{:S(2)}) async-start(), calls=%async_computation.5 | async-start | bytes 262144 | tf_op jit(solution)/shard_map/psum | solution.py:39
  472.3 2.4 copy-start.2
  474.8 3.1 copy-start.8
  476.9 1.0 copy-start.4
  483.6 39.5 %copy-start.11 = (f32[8,16,256]{2,1,0:T(8,128)S(1)}, f32[8,16,256]{2,1,0:T(8,128)}, u32[]{:S(2)}) copy-start(f32[8,16,256]{2,1,0:T(8,128)} %all-reduce.14.cloned.1.call-done) | copy-start | bytes 393220
Sparse Core Ops, SparseCore 0:
  13.9 45.8 all-reduce.21
  65.4 65.1 all-reduce.9
  135.5 42.6 all-reduce.11
  248.9 42.2 all-reduce.13
  297.2 65.0 all-reduce.15
  367.2 42.6 all-reduce.17
  480.9 42.1 all-reduce.19
where the time goes:
time: 538 us; the launch traced here: 532 us
  waiting for transfers between devices  335 us (62%)
  other arithmetic  116 us (22%)
  matrix products  41.7 us (8%)
  local copies, waits for them, and re-layouts  21.9 us (4%)
  between operations  17.3 us (3%)
    psum x2, waiting for transfers between devices, refresh(): total = lax.psum(local_sum, 'tenant')  130 us
    psum x2, waiting for transfers between devices, refresh(): gram = lax.psum(jnp.dot(total.T, total, precision=HIGH), 'row')  79.4 us
    another operation x13, other arithmetic, normalize(): lower = jnp.linalg.cholesky(gram)  68.5 us
    psum x1, waiting for transfers between devices, local(): lax.psum((project(b_factors, u_start), project(a_factors, v_start)), 'row')  45.9 us
    psum x1, waiting for transfers between devices, local(): left = lax.psum(project(b_factors, basis_u), 'row')  42.3 us
    another operation x5, other arithmetic, normalize(): lax.linalg.triangular_solve(lower, matrix, left_side=False, lower=True, t...  39.6 us
    psum x1, waiting for transfers between devices, local(): right = lax.psum(project(a_factors, basis_v), 'row')  36.6 us
    unnamed x28, local copies, waits for them, and re-layouts  11.7 us
  transfers between devices with their start and end apart: 7, of which 7 were waited for; matrix products, arithmetic and copies ran while one was open for 2% of the time, Pallas kernels for 0%

commit v1 on v0

v1 whole, which is shorter than its diff:
```python
import functools
import math

import jax
import jax.numpy as jnp
from jax import lax
from jax.experimental import pallas as pl
from jax.experimental.pallas import tpu as pltpu
from jax.sharding import PartitionSpec as P

HIGH = lax.Precision.HIGHEST
MESH = pl.DeviceIdType.MESH
VMEM = pl.BlockSpec(memory_space=pltpu.VMEM)
LANES = 128
BLK = 64


def mm(x, y, cx, cy):
    return lax.dot_general(x, y, (((cx,), (cy,)), ((), ())), precision=HIGH, preferred_element_type=jnp.float32)


def remote(src, dst, send, recv, device):
    return pltpu.make_async_remote_copy(
        src_ref=src, dst_ref=dst, send_sem=send, recv_sem=recv, device_id=device, device_id_type=MESH)


def signal(device):
    pl.semaphore_signal(pltpu.get_barrier_semaphore(), inc=1, device_id=device, device_id_type=MESH)


def bits_of(n_row):
    bits = n_row.bit_length() - 1
    assert 1 << bits == n_row
    return bits


def row_partner(bit):
    row = lax.axis_index("row")
    return row + (1 << bit) - 2 * (1 << bit) * (lax.rem(row // (1 << bit), 2))


def row_sum(bits, acc, got, send, recv):
    half = acc.shape[1] // 2

    def copy(step, part):
        bit = (step + part) % bits
        rows = pl.ds(part * half, half)
        return remote(acc.at[step, rows], got.at[step, rows], send.at[step, part], recv.at[step, part],
                      {"row": row_partner(bit)})

    for part in range(2):
        copy(0, part).start()
    for step in range(bits):
        for part in range(2):
            rows = pl.ds(part * half, half)
            copy(step, part).wait_recv()
            acc[step + 1, rows, :] = acc[step, rows, :] + got[step, rows, :]
            if step + 1 < bits:
                copy(step + 1, part).start()
    for step in range(bits):
        for part in range(2):
            copy(step, part).wait_send()


def start_kernel(bits, b_ref, a_ref, u_ref, v_ref, out_ref, acc, got, send, recv):
    for bit in range(bits):
        signal({"row": row_partner(bit)})
    rows, width = b_ref.shape
    tile = 512 if width % 512 == 0 else width
    acc[0] = jnp.zeros_like(acc[0])

    def step(i, _):
        cols = pl.ds(pl.multiple_of(i * tile, tile), tile)
        acc[0, :rows, :] += mm(b_ref[:, cols], u_ref[cols, :], 1, 0)
        acc[0, rows:, :] += mm(a_ref[:, cols], v_ref[cols, :], 1, 0)
        return 0

    lax.fori_loop(0, width // tile, step, 0)
    pl.semaphore_wait(pltpu.get_barrier_semaphore(), bits)
    row_sum(bits, acc, got, send, recv)
    out_ref[...] = acc[bits]


def start(bits, b, a, u, v):
    rows, k = b.shape[0], u.shape[1]
    return pl.pallas_call(
        functools.partial(start_kernel, bits),
        out_shape=jax.ShapeDtypeStruct((2 * rows, k), jnp.float32),
        in_specs=[VMEM] * 4,
        out_specs=VMEM,
        scratch_shapes=[
            pltpu.VMEM((bits + 1, 2 * rows, k), jnp.float32),
            pltpu.VMEM((bits, 2 * rows, k), jnp.float32),
            pltpu.SemaphoreType.DMA((bits, 2)),
            pltpu.SemaphoreType.DMA((bits, 2)),
        ],
        compiler_params=pltpu.CompilerParams(collective_id=0, has_side_effects=True),
    )(b, a, u, v)


def refresh_kernel(bits, chain, rank, f_ref, x_ref, y_ref, m_ref, s_ref, other, pair, up, got, acc, rgot, coeff,
                   pair_send, pair_recv, in_send, recv, out_send, fin_send, fin_recv, row_send, row_recv):
    tenant = lax.axis_index("tenant")
    core = lax.rem(tenant, 2)
    place = tenant // 2
    nch = other.shape[0]
    lower = (place < chain // 2).astype(jnp.int32)
    toward = 2 * lower - 1
    mate = {"tenant": tenant + 1 - 2 * core}
    inner = {"tenant": tenant + 2 * toward}
    dist = lower * (chain // 2 - 1 - place) + (1 - lower) * (place - chain // 2)
    mid = (dist == 0).astype(jnp.int32)
    is_end = dist == chain // 2 - 1
    outer = {"tenant": jnp.where(is_end, tenant, tenant - 2 * toward)}

    signal(mate)
    signal(inner)
    for bit in range(bits):
        signal({"row": row_partner(bit)})

    @pl.when(jnp.logical_not(is_end))
    def _():
        signal(outer)

    rows, width = f_ref.shape
    half = width // 2
    tile = other.shape[1]
    weight = mm(x_ref[...], x_ref[...], 1, 1)
    same = lax.broadcasted_iota(jnp.int32, weight.shape, 0) // rank == lax.broadcasted_iota(
        jnp.int32, weight.shape, 1) // rank
    coeff[...] = mm(jnp.where(same, weight, 0.0), y_ref[...], 1, 0)
    pl.semaphore_wait(pltpu.get_barrier_semaphore(), 3 + bits - is_end.astype(jnp.int32))

    def rows_of(side, ch):
        return pl.ds(pl.multiple_of(side * half + ch * tile, tile), tile)

    def term(side, ch):
        return mm(f_ref[:, rows_of(side, ch)], coeff[...], 0, 0)

    def pair_copy(ch):
        return remote(other.at[ch], pair.at[ch], pair_send.at[ch], pair_recv.at[ch], mate)

    def in_copy(ch, slot):
        return remote(up.at[ch], got.at[slot, ch], in_send.at[ch], recv.at[slot, ch], inner)

    def out_copy(ch):
        mine = m_ref.at[rows_of(core, ch)]
        return remote(mine, got.at[1, ch], out_send.at[ch], recv.at[1, ch], outer)

    def fin_copy(side, ch):
        part = m_ref.at[rows_of(side, ch)]
        return remote(part, part, fin_send.at[ch], fin_recv.at[ch], mate)

    acc[0] = jnp.zeros_like(acc[0])

    def first(ch, _):
        other[ch] = term(1 - core, ch)
        pair_copy(ch).start()
        return 0

    lax.fori_loop(0, nch, first, 0)

    def gather_up(ch):
        up[ch] = term(core, ch)
        pair_copy(ch).wait_recv()
        up[ch] += pair[ch]

        @pl.when(jnp.logical_not(is_end))
        def _():
            in_copy(ch, 0).wait_recv()
            up[ch] += got[0, ch]

        in_copy(ch, mid).start()

    def accumulate(ch):
        fin_copy(1 - core, ch).wait_recv()
        for side in range(2):
            block = m_ref[rows_of(side, ch), :]
            acc[0, :rows, :] += mm(f_ref[:, rows_of(side, ch)], block, 1, 0)
            acc[0, rows:, :] += mm(block, block, 0, 0)

    def settle(ch):
        in_copy(ch, 1).wait_recv()

        @pl.when(mid == 1)
        def _():
            m_ref[rows_of(core, ch), :] = up[ch] + got[1, ch]

        @pl.when(mid == 0)
        def _():
            m_ref[rows_of(core, ch), :] = got[1, ch]

        @pl.when(jnp.logical_not(is_end))
        def _():
            out_copy(ch).start()

        fin_copy(core, ch).start()

        @pl.when(ch > 0)
        def _():
            accumulate(ch - 1)

    lag = 1 + 4 * dist

    def step(i, _):
        @pl.when(i < nch)
        def _():
            gather_up(i)

        @pl.when(jnp.logical_and(i >= lag, i < nch + lag))
        def _():
            settle(i - lag)

        return 0

    lax.fori_loop(0, nch + 1 + 4 * (chain // 2 - 1), step, 0)
    accumulate(nch - 1)
    row_sum(bits, acc, rgot, row_send, row_recv)
    s_ref[...] = acc[bits]

    def drain(ch, _):
        pair_copy(ch).wait_send()
        in_copy(ch, mid).wait_send()
        fin_copy(core, ch).wait_send()

        @pl.when(jnp.logical_not(is_end))
        def _():
            out_copy(ch).wait_send()

        return 0

    lax.fori_loop(0, nch, drain, 0)


def refresh(bits, chain, rank, f, x, y):
    rows, width = f.shape
    k = x.shape[1]
    tile = min(LANES, width // 2)
    nch = width // 2 // tile
    f32 = jnp.float32
    dma = pltpu.SemaphoreType.DMA
    return pl.pallas_call(
        functools.partial(refresh_kernel, bits, chain, rank),
        out_shape=(jax.ShapeDtypeStruct((width, k), f32), jax.ShapeDtypeStruct((rows + k, k), f32)),
        in_specs=[VMEM] * 3,
        out_specs=(VMEM, VMEM),
        scratch_shapes=[
            pltpu.VMEM((nch, tile, k), f32),
            pltpu.VMEM((nch, tile, k), f32),
            pltpu.VMEM((nch, tile, k), f32),
            pltpu.VMEM((2, nch, tile, k), f32),
            pltpu.VMEM((bits + 1, rows + k, k), f32),
            pltpu.VMEM((bits, rows + k, k), f32),
            pltpu.VMEM((rows, k), f32),
            dma((nch,)), dma((nch,)), dma((nch,)), dma((2, nch)), dma((nch,)), dma((nch,)), dma((nch,)),
            dma((bits, 2)), dma((bits, 2)),
        ],
        compiler_params=pltpu.CompilerParams(collective_id=1, has_side_effects=True),
    )(f, x, y)


def factor_block(block):
    n = block.shape[0]
    eye = (lax.broadcasted_iota(jnp.int32, (n, n), 0) == lax.broadcasted_iota(jnp.int32, (n, n), 1)).astype(block.dtype)
    full = jnp.concatenate([block, eye], axis=1)
    groups = [full[8 * g:8 * g + 8, :] for g in range(n // 8)]
    sub = lax.broadcasted_iota(jnp.int32, (8, 1), 0)
    for j in range(n):
        g, s = j // 8, j % 8
        row = groups[g][s:s + 1, :]
        inv = 1.0 / row[:, j:j + 1]
        scaled = row * inv
        for h in range(g, n // 8):
            col = groups[h][:, j:j + 1]
            if h == g:
                col = jnp.where(sub > s, col, 0.0)
            groups[h] = groups[h] - col * scaled
    full = jnp.concatenate(groups, axis=0)
    diag = jnp.sum(full[:, :n] * eye, axis=1, keepdims=True)
    return full[:, n:] * lax.rsqrt(diag)


def factor_kernel(s_ref, inv_ref, left_ref, tab):
    k = inv_ref.shape[0]
    rows = left_ref.shape[0]
    tab[:, :k] = s_ref[rows:, :]
    tab[:, k:] = (lax.broadcasted_iota(jnp.int32, (k, k), 0) == lax.broadcasted_iota(
        jnp.int32, (k, k), 1)).astype(jnp.float32)
    for at in range(0, k, BLK):
        end = at + BLK
        small = factor_block(tab[at:end, at:end])
        done = mm(small, tab[at:end, :], 1, 0)
        tab[at:end, :] = done
        if end < k:
            tab[end:, :] -= mm(done[:, end:k], done, 0, 0)
    inv_ref[...] = tab[:, k:]
    left_ref[...] = mm(s_ref[:rows, :], tab[:, k:], 1, 1)


def factor(s):
    k = s.shape[1]
    rows = s.shape[0] - k
    return pl.pallas_call(
        factor_kernel,
        out_shape=(jax.ShapeDtypeStruct((k, k), jnp.float32), jax.ShapeDtypeStruct((rows, k), jnp.float32)),
        in_specs=[VMEM],
        out_specs=(VMEM, VMEM),
        scratch_shapes=[pltpu.VMEM((k, 2 * k), jnp.float32)],
    )(s)


def local(mesh_shape, b_factors, a_factors, u_start, v_start):
    nt, rank, width = b_factors.shape
    rows = nt * rank
    k = u_start.shape[1]
    bits = bits_of(mesh_shape["row"])
    chain = mesh_shape["tenant"] // 2
    b = b_factors.reshape(rows, width)
    a = a_factors.reshape(rows, width)
    both = start(bits, b, a, u_start, v_start)
    left, right = both[:rows], both[rows:]
    basis_u, sums = refresh(bits, chain, rank, b, right, left)
    inv_u, left = factor(sums)
    basis_v, sums = refresh(bits, chain, rank, a, left, right)
    inv_v, right = factor(sums)
    scale = math.sqrt(width * mesh_shape["row"])
    u = mm(basis_u, inv_u * scale, 1, 1)
    v = mm(basis_v, inv_v * scale, 1, 1)
    return u, v, left.reshape(nt, rank, k), right.reshape(nt, rank, k)


def solution(mesh):
    in_specs = (P("tenant", None, "row"), P("tenant", None, "row"), P("row", None), P("row", None))
    out_specs = (P("row", None), P("row", None), P("tenant", None, None), P("tenant", None, None))
    return jax.shard_map(functools.partial(local, dict(mesh.shape)), mesh=mesh, in_specs=in_specs,
                         out_specs=out_specs, check_vma=False)
```

time: 538 us -> 196 us (0.36)
  waiting for transfers between devices: 335 us -> 0 us
  Pallas kernels: 0 us -> 184 us
  other arithmetic: 116 us -> 0 us
  matrix products: 41.7 us -> 9.49 us
  local copies, waits for them, and re-layouts: 21.9 us -> 1.68 us
  between operations: 17.3 us -> 0.66 us
    psum x7 -> x0, waiting for transfers between devices: 335 us -> none  [the longest x2 130 us: refresh(): total = lax.psum(local_sum, 'tenant')]
    pallas_call x0 -> x5, Pallas kernels: none -> 184 us  [the longest x2 114 us: refresh(): pl.pallas_call(functools.partial(refresh_kernel, bits, chain, rank), out_...]
    another operation x18 -> x0, other arithmetic: 108 us -> none  [the longest x13 68.5 us: normalize(): lower = jnp.linalg.cholesky(gram)]
    dot_general x12 -> x2, matrix products: 31.7 us -> 9.49 us  [mm(): lax.dot_general(x, y, (((cx,), (cy,)), ((), ())), precision=HIGH, preferr...]
    unnamed x28 -> x0, local copies, waits for them, and re-layouts: 11.7 us -> none
    another operation x10 -> x0, matrix products: 10 us -> none  [the longest x6 9.1 us: normalize(): lax.linalg.triangular_solve(lower, matrix, left_side=False, lower=True, t...]
    another operation x19 -> x0, local copies, waits for them, and re-layouts: 8.04 us -> none  [the longest x15 7.99 us: normalize(): lax.linalg.triangular_solve(lower, matrix, left_side=False, lower=True, t...]
    mul x2 -> x0, other arithmetic: 5.69 us -> none  [local(): return (basis_u * scale, basis_v * scale, left, right)]
  transfers between devices with their start and end apart: 7 -> 0, of which waited for: 7 -> 0; matrix products, arithmetic and copies ran while one was open for 2% -> 0% of each run, Pallas kernels for 0% -> 0%
where the time goes in v1:
time: 196 us; the launch traced here: 195 us
  Pallas kernels  184 us (94%)
  matrix products  9.49 us (5%)
    pallas_call x2, Pallas kernels, refresh(): pl.pallas_call(functools.partial(refresh_kernel, bits, chain, rank), out_...  114 us
    pallas_call x2, Pallas kernels, factor(): pl.pallas_call(factor_kernel, out_shape=(jax.ShapeDtypeStruct((k, k), jnp...  52.5 us
    pallas_call x1, Pallas kernels, start(): pl.pallas_call(functools.partial(start_kernel, bits), out_shape=jax.Shape...  17.6 us
    dot_general x2, matrix products, mm(): lax.dot_general(x, y, (((cx,), (cy,)), ((), ())), precision=HIGH, preferr...  9.49 us

profile of v1, /device:TPU:0, one launch (start us, length us, event | category | flops | bytes accessed | tf_op | source)
XLA Modules:
  0.0 195.5 jit_solution(6651109336277302459)
XLA Ops:
  0.6 17.6 %shard_map.75 = f32[256,256]{1,0:T(8,128)} custom-call(f32[128,2048]{1,0:T(8,128)} %bitcast.6, f32[128,2048]{1,0:T(8,128)} %bitcast.8, f32[2048,256]{1,0:T(8,128)} %u_ref.1, f32[2048,256]{1,0:T(8,128)} %v_ref.1), custom_call_target="tpu_custom_call" | custom-call | tf_op jit(solution)/shard_map/pallas_call | solution.py:86
  18.2 1.7 fusion.8
  19.9 57.3 %shard_map.76 = (f32[2048,256]{1,0:T(8,128)}, f32[384,256]{1,0:T(8,128)}) custom-call(f32[128,2048]{1,0:T(8,128)} %bitcast.7, f32[128,256]{1,0:T(8,128)} %get-tuple-element.21.x_ref.y_ref, f32[128,256]{1,0:T(8,128)} %get-tuple-element.20.y_ref), custom_call_target="tpu_custom_call" | custom-call | tf_op jit(solution)/shard_map/pallas_call | solution.py:242
  77.1 26.2 %shard_map.77 = (f32[256,256]{1,0:T(8,128)}, f32[128,256]{1,0:T(8,128)}) custom-call(f32[384,256]{1,0:T(8,128)} %get-tuple-element.13.s_ref), custom_call_target="tpu_custom_call" | custom-call | tf_op jit(solution)/shard_map/pallas_call | solution.py:303
  103.4 4.7 %fusion.2 = f32[2048,256]{1,0:T(8,128)} fusion(f32[2048,256]{1,0:T(8,128)} %get-tuple-element.12, f32[256,256]{1,0:T(8,128)} %get-tuple-element.14), kind=kOutput, calls=%fused_computation.2 | convolution fusion | flops 1610678272 | bytes 4456448 | tf_op jit(solution)/shard_map/dot_general | solution.py:19
  108.1 56.3 %shard_map.78 = (f32[2048,256]{1,0:T(8,128)}, f32[384,256]{1,0:T(8,128)}) custom-call(f32[128,2048]{1,0:T(8,128)} %bitcast.9, f32[128,256]{1,0:T(8,128)} %get-tuple-element.15.x_ref, f32[128,256]{1,0:T(8,128)} %get-tuple-element.21.x_ref.y_ref), custom_call_target="tpu_custom_call" | custom-call | tf_op jit(solution)/shard_map/pallas_call | solution.py:242
  164.5 26.2 %shard_map.79 = (f32[256,256]{1,0:T(8,128)}, f32[128,256]{1,0:T(8,128)}) custom-call(f32[384,256]{1,0:T(8,128)} %get-tuple-element.17.s_ref), custom_call_target="tpu_custom_call" | custom-call | tf_op jit(solution)/shard_map/pallas_call | solution.py:303
  190.7 4.7 %fusion = f32[2048,256]{1,0:T(8,128)} fusion(f32[2048,256]{1,0:T(8,128)} %get-tuple-element.16, f32[256,256]{1,0:T(8,128)} %get-tuple-element.18), kind=kOutput, calls=%fused_computation | convolution fusion | flops 1610678272 | bytes 4456448 | tf_op jit(solution)/shard_map/dot_general | solution.py:19

commit v2 on v1

--- a/solution.py
+++ b/solution.py
@@ -17,6 +17,18 @@
 
 def mm(x, y, cx, cy):
     return lax.dot_general(x, y, (((cx,), (cy,)), ((), ())), precision=HIGH, preferred_element_type=jnp.float32)
+
+
+def split(x):
+    top = x.astype(jnp.bfloat16)
+    return top, (x - top.astype(jnp.float32)).astype(jnp.bfloat16)
+
+
+def mm3(x, y, cx, cy):
+    (xt, xl), (yt, yl) = split(x), split(y)
+    dot = functools.partial(lax.dot_general, dimension_numbers=(((cx,), (cy,)), ((), ())),
+                            preferred_element_type=jnp.float32)
+    return dot(xt, yt) + (dot(xt, yl) + dot(xl, yt))
 
 
 def remote(src, dst, send, recv, device):
@@ -71,8 +83,8 @@
 
     def step(i, _):
         cols = pl.ds(pl.multiple_of(i * tile, tile), tile)
-        acc[0, :rows, :] += mm(b_ref[:, cols], u_ref[cols, :], 1, 0)
-        acc[0, rows:, :] += mm(a_ref[:, cols], v_ref[cols, :], 1, 0)
+        acc[0, :rows, :] += mm3(b_ref[:, cols], u_ref[cols, :], 1, 0)
+        acc[0, rows:, :] += mm3(a_ref[:, cols], v_ref[cols, :], 1, 0)
         return 0
 
     lax.fori_loop(0, width // tile, step, 0)
@@ -99,7 +111,7 @@
 
 
 def refresh_kernel(bits, chain, rank, f_ref, x_ref, y_ref, m_ref, s_ref, other, pair, up, got, acc, rgot, coeff,
-                   pair_send, pair_recv, in_send, recv, out_send, fin_send, fin_recv, row_send, row_recv):
+                   pair_send, pair_recv, in_send, recv, out_send, fin_send, fin_recv, row_send, row_recv, gram_send, gram_recv):
     tenant = lax.axis_index("tenant")
     core = lax.rem(tenant, 2)
     place = tenant // 2
@@ -135,7 +147,7 @@
         return pl.ds(pl.multiple_of(side * half + ch * tile, tile), tile)
 
     def term(side, ch):
-        return mm(f_ref[:, rows_of(side, ch)], coeff[...], 0, 0)
+        return mm3(f_ref[:, rows_of(side, ch)], coeff[...], 0, 0)
 
     def pair_copy(ch):
         return remote(other.at[ch], pair.at[ch], pair_send.at[ch], pair_recv.at[ch], mate)
@@ -172,12 +184,15 @@
 
         in_copy(ch, mid).start()
 
+    k = m_ref.shape[1]
+    part = pl.ds(pl.multiple_of(core * (k // 2), k // 2), k // 2)
+
     def accumulate(ch):
         fin_copy(1 - core, ch).wait_recv()
         for side in range(2):
             block = m_ref[rows_of(side, ch), :]
-            acc[0, :rows, :] += mm(f_ref[:, rows_of(side, ch)], block, 1, 0)
-            acc[0, rows:, :] += mm(block, block, 0, 0)
+            acc[0, :rows, :] += mm3(f_ref[:, rows_of(side, ch)], block, 1, 0)
+            acc[0, rows:, :] += mm(m_ref[rows_of(side, ch), part], block, 0, 0)
 
     def settle(ch):
         in_copy(ch, 1).wait_recv()
@@ -216,7 +231,14 @@
     lax.fori_loop(0, nch + 1 + 4 * (chain // 2 - 1), step, 0)
     accumulate(nch - 1)
     row_sum(bits, acc, rgot, row_send, row_recv)
-    s_ref[...] = acc[bits]
+    s_ref[:rows, :] = acc[bits, :rows, :]
+
+    def gram_copy(side):
+        here = s_ref.at[pl.ds(pl.multiple_of(rows + side * (k // 2), 8), k // 2)]
+        return remote(here, here, gram_send, gram_recv, mate)
+
+    s_ref[pl.ds(pl.multiple_of(rows + core * (k // 2), 8), k // 2), :] = acc[bits, rows:, :]
+    gram_copy(core).start()
 
     def drain(ch, _):
         pair_copy(ch).wait_send()
@@ -230,6 +252,8 @@
         return 0
 
     lax.fori_loop(0, nch, drain, 0)
+    gram_copy(1 - core).wait_recv()
+    gram_copy(core).wait_send()
 
 
 def refresh(bits, chain, rank, f, x, y):
@@ -249,11 +273,11 @@
             pltpu.VMEM((nch, tile, k), f32),
             pltpu.VMEM((nch, tile, k), f32),
             pltpu.VMEM((2, nch, tile, k), f32),
-            pltpu.VMEM((bits + 1, rows + k, k), f32),
-            pltpu.VMEM((bits, rows + k, k), f32),
+            pltpu.VMEM((bits + 1, rows + k // 2, k), f32),
+            pltpu.VMEM((bits, rows + k // 2, k), f32),
             pltpu.VMEM((rows, k), f32),
             dma((nch,)), dma((nch,)), dma((nch,)), dma((2, nch)), dma((nch,)), dma((nch,)), dma((nch,)),
-            dma((bits, 2)), dma((bits, 2)),
+            dma((bits, 2)), dma((bits, 2)), dma(()), dma(()),
         ],
         compiler_params=pltpu.CompilerParams(collective_id=1, has_side_effects=True),
     )(f, x, y)
@@ -264,17 +288,34 @@
     eye = (lax.broadcasted_iota(jnp.int32, (n, n), 0) == lax.broadcasted_iota(jnp.int32, (n, n), 1)).astype(block.dtype)
     full = jnp.concatenate([block, eye], axis=1)
     groups = [full[8 * g:8 * g + 8, :] for g in range(n // 8)]
-    sub = lax.broadcasted_iota(jnp.int32, (8, 1), 0)
-    for j in range(n):
-        g, s = j // 8, j % 8
-        row = groups[g][s:s + 1, :]
-        inv = 1.0 / row[:, j:j + 1]
-        scaled = row * inv
-        for h in range(g, n // 8):
-            col = groups[h][:, j:j + 1]
-            if h == g:
-                col = jnp.where(sub > s, col, 0.0)
-            groups[h] = groups[h] - col * scaled
+    sub = lax.broadcasted_iota(jnp.int32, (8, 2 * n), 0)
+    for g in range(n // 8):
+        cols = [[jnp.broadcast_to(groups[h][:, 8 * g + c:8 * g + c + 1], (8, 2 * n)) for c in range(8)]
+                for h in range(g, n // 8)]
+        heads = [[cols[0][c][r:r + 1, :] for c in range(8)] for r in range(8)]
+        lines = [groups[g][r:r + 1, :] for r in range(8)]
+        invs = []
+        for p in range(8):
+            inv = 1.0 / heads[p][p]
+            invs.append(inv)
+            for r in range(p + 1, 8):
+                factor = heads[r][p] * inv
+                lines[r] = lines[r] - factor * lines[p]
+                for c in range(p + 1, 8):
+                    heads[r][c] = heads[r][c] - factor * heads[p][c]
+        for h in range(g + 1, n // 8):
+            col = cols[h - g]
+            total = groups[h]
+            for p in range(8):
+                factor = col[p] * invs[p]
+                total = total - factor * lines[p]
+                for c in range(p + 1, 8):
+                    col[c] = col[c] - factor * heads[p][c]
+            groups[h] = total
+        group = jnp.broadcast_to(lines[0], (8, 2 * n))
+        for r in range(1, 8):
+            group = jnp.where(sub == r, lines[r], group)
+        groups[g] = group
     full = jnp.concatenate(groups, axis=0)
     diag = jnp.sum(full[:, :n] * eye, axis=1, keepdims=True)
     return full[:, n:] * lax.rsqrt(diag)
@@ -309,6 +350,10 @@
     )(s)
 
 
+def finish(basis, inv):
+    return lax.dot_general(basis, inv, (((1,), (1,)), ((), ())), precision=lax.Precision.HIGH)
+
+
 def local(mesh_shape, b_factors, a_factors, u_start, v_start):
     nt, rank, width = b_factors.shape
     rows = nt * rank
@@ -324,8 +369,8 @@
     basis_v, sums = refresh(bits, chain, rank, a, left, right)
     inv_v, right = factor(sums)
     scale = math.sqrt(width * mesh_shape["row"])
-    u = mm(basis_u, inv_u * scale, 1, 1)
-    v = mm(basis_v, inv_v * scale, 1, 1)
+    u = finish(basis_u, inv_u * scale)
+    v = finish(basis_v, inv_v * scale)
     return u, v, left.reshape(nt, rank, k), right.reshape(nt, rank, k)
 
 

time: 196 us -> 157 us (0.80)
  Pallas kernels: 184 us -> 147 us
    pallas_call x2, Pallas kernels: 52.5 us -> 23.6 us  [factor(): pl.pallas_call(factor_kernel, out_shape=(jax.ShapeDtypeStruct((k, k), jnp...]
    pallas_call x2, Pallas kernels: 114 us -> 107 us  [refresh(): pl.pallas_call(functools.partial(refresh_kernel, bits, chain, rank), out_...]
where the time goes in v2:
time: 157 us
  Pallas kernels  147 us (94%)
  matrix products  7.89 us (5%)
  local copies, waits for them, and re-layouts  1.68 us (1%)
    pallas_call x2, Pallas kernels, refresh(): pl.pallas_call(functools.partial(refresh_kernel, bits, chain, rank), out_...  107 us
    pallas_call x2, Pallas kernels, factor(): pl.pallas_call(factor_kernel, out_shape=(jax.ShapeDtypeStruct((k, k), jnp...  23.6 us
    pallas_call x1, Pallas kernels, start(): pl.pallas_call(functools.partial(start_kernel, bits), out_shape=jax.Shape...  16.4 us
    dot_general x2, matrix products, finish(): lax.dot_general(basis, inv, (((1,), (1,)), ((), ())), precision=lax.Preci...  7.89 us

profile of v2, /device:TPU:0, one launch (start us, length us, event | category | flops | bytes accessed | tf_op | source)
XLA Modules:
  0.0 156.8 jit_solution(1432497354080918206)
XLA Ops:
  0.6 16.4 %shard_map.75 = f32[256,256]{1,0:T(8,128)} custom-call(f32[128,2048]{1,0:T(8,128)} %bitcast.6, f32[128,2048]{1,0:T(8,128)} %bitcast.8, f32[2048,256]{1,0:T(8,128)} %u_ref.1, f32[2048,256]{1,0:T(8,128)} %v_ref.1), custom_call_target="tpu_custom_call" | custom-call | tf_op jit(solution)/shard_map/pallas_call | solution.py:98
  17.0 1.7 %fusion.8 = (f32[128,256]{1,0:T(8,128)}, f32[128,256]{1,0:T(8,128)}) fusion(f32[256,256]{1,0:T(8,128)} %shard_map.75), kind=kLoop, calls=%fused_computation.8 | loop fusion | bytes 524288 | tf_op jit(solution)/shard_map/slice | solution.py:366
  18.7 53.9 %shard_map.76 = (f32[2048,256]{1,0:T(8,128)}, f32[384,256]{1,0:T(8,128)}) custom-call(f32[128,2048]{1,0:T(8,128)} %bitcast.7, f32[128,256]{1,0:T(8,128)} %get-tuple-element.21.x_ref.y_ref, f32[128,256]{1,0:T(8,128)} %get-tuple-element.20.y_ref), custom_call_target="tpu_custom_call" | custom-call | tf_op jit(solution)/shard_map/pallas_call | solution.py:266
  72.6 11.8 %shard_map.77 = (f32[256,256]{1,0:T(8,128)}, f32[128,256]{1,0:T(8,128)}) custom-call(f32[384,256]{1,0:T(8,128)} %get-tuple-element.13.s_ref), custom_call_target="tpu_custom_call" | custom-call | tf_op jit(solution)/shard_map/pallas_call | solution.py:344
  84.4 3.9 %fusion.2 = f32[2048,256]{1,0:T(8,128)} fusion(f32[2048,256]{1,0:T(8,128)} %get-tuple-element.12, f32[256,256]{1,0:T(8,128)} %get-tuple-element.14), kind=kOutput, calls=%fused_computation.2 | convolution fusion | flops 805371904 | bytes 4456448 | tf_op jit(solution)/shard_map/dot_general | solution.py:354
  88.3 52.7 %shard_map.78 = (f32[2048,256]{1,0:T(8,128)}, f32[384,256]{1,0:T(8,128)}) custom-call(f32[128,2048]{1,0:T(8,128)} %bitcast.9, f32[128,256]{1,0:T(8,128)} %get-tuple-element.15.x_ref, f32[128,256]{1,0:T(8,128)} %get-tuple-element.21.x_ref.y_ref), custom_call_target="tpu_custom_call" | custom-call | tf_op jit(solution)/shard_map/pallas_call | solution.py:266
  141.0 11.8 %shard_map.79 = (f32[256,256]{1,0:T(8,128)}, f32[128,256]{1,0:T(8,128)}) custom-call(f32[384,256]{1,0:T(8,128)} %get-tuple-element.17.s_ref), custom_call_target="tpu_custom_call" | custom-call | tf_op jit(solution)/shard_map/pallas_call | solution.py:344
  152.8 3.9 %fusion = f32[2048,256]{1,0:T(8,128)} fusion(f32[2048,256]{1,0:T(8,128)} %get-tuple-element.16, f32[256,256]{1,0:T(8,128)} %get-tuple-element.18), kind=kOutput, calls=%fused_computation | convolution fusion | flops 805371904 | bytes 4456448 | tf_op jit(solution)/shard_map/dot_general | solution.py:354

commit v3 on v2

--- a/solution.py
+++ b/solution.py
@@ -51,60 +51,96 @@
     return row + (1 << bit) - 2 * (1 << bit) * (lax.rem(row // (1 << bit), 2))
 
 
-def row_sum(bits, acc, got, send, recv):
-    half = acc.shape[1] // 2
+def row_parts(bits, acc, got, send, recv, base, size):
+    half = size // 2
 
     def copy(step, part):
         bit = (step + part) % bits
-        rows = pl.ds(part * half, half)
-        return remote(acc.at[step, rows], got.at[step, rows], send.at[step, part], recv.at[step, part],
+        rows = pl.ds(base + part * half, half)
+        at = base // size
+        return remote(acc.at[step, rows], got.at[step, rows], send.at[at, step, part], recv.at[at, step, part],
                       {"row": row_partner(bit)})
 
-    for part in range(2):
-        copy(0, part).start()
-    for step in range(bits):
+    def begin():
         for part in range(2):
-            rows = pl.ds(part * half, half)
+            copy(0, part).start()
+
+    def meet(step):
+        for part in range(2):
+            rows = pl.ds(base + part * half, half)
             copy(step, part).wait_recv()
             acc[step + 1, rows, :] = acc[step, rows, :] + got[step, rows, :]
             if step + 1 < bits:
                 copy(step + 1, part).start()
+
+    def end():
+        for step in range(bits):
+            for part in range(2):
+                copy(step, part).wait_send()
+
+    return begin, meet, end
+
+
+def row_sum(bits, acc, got, send, recv):
+    begin, meet, end = row_parts(bits, acc, got, send, recv, 0, acc.shape[1])
+    begin()
     for step in range(bits):
-        for part in range(2):
-            copy(step, part).wait_send()
-
-
-def start_kernel(bits, b_ref, a_ref, u_ref, v_ref, out_ref, acc, got, send, recv):
+        meet(step)
+    end()
+
+
+def start_kernel(bits, b_hbm, a_hbm, u_hbm, v_hbm, left_ref, right_ref, b_ref, a_ref, u_ref, v_ref, acc, got,
+                 load, send, recv):
+    pairs = ((b_hbm, b_ref), (u_hbm, u_ref), (a_hbm, a_ref), (v_hbm, v_ref))
+    loads = [pltpu.make_async_copy(src, dst, load.at[i]) for i, (src, dst) in enumerate(pairs)]
+    for copy in loads:
+        copy.start()
     for bit in range(bits):
         signal({"row": row_partner(bit)})
     rows, width = b_ref.shape
     tile = 512 if width % 512 == 0 else width
     acc[0] = jnp.zeros_like(acc[0])
-
-    def step(i, _):
-        cols = pl.ds(pl.multiple_of(i * tile, tile), tile)
-        acc[0, :rows, :] += mm3(b_ref[:, cols], u_ref[cols, :], 1, 0)
-        acc[0, rows:, :] += mm3(a_ref[:, cols], v_ref[cols, :], 1, 0)
-        return 0
-
-    lax.fori_loop(0, width // tile, step, 0)
-    pl.semaphore_wait(pltpu.get_barrier_semaphore(), bits)
-    row_sum(bits, acc, got, send, recv)
-    out_ref[...] = acc[bits]
+    parts = [row_parts(bits, acc, got, send, recv, side * rows, rows) for side in range(2)]
+    for side, (factors, basis) in enumerate(((b_ref, u_ref), (a_ref, v_ref))):
+        loads[2 * side].wait()
+        loads[2 * side + 1].wait()
+
+        def step(i, _, side=side, factors=factors, basis=basis):
+            cols = pl.ds(pl.multiple_of(i * tile, tile), tile)
+            acc[0, pl.ds(side * rows, rows), :] += mm3(factors[:, cols], basis[cols, :], 1, 0)
+            return 0
+
+        lax.fori_loop(0, width // tile, step, 0)
+        if side == 0:
+            pl.semaphore_wait(pltpu.get_barrier_semaphore(), bits)
+        parts[side][0]()
+    for step in range(bits):
+        for side in range(2):
+            parts[side][1](step)
+    for side in range(2):
+        parts[side][2]()
+    left_ref[...] = acc[bits, :rows, :]
+    right_ref[...] = acc[bits, rows:, :]
 
 
 def start(bits, b, a, u, v):
     rows, k = b.shape[0], u.shape[1]
+    out = jax.ShapeDtypeStruct((rows, k), jnp.float32)
     return pl.pallas_call(
         functools.partial(start_kernel, bits),
-        out_shape=jax.ShapeDtypeStruct((2 * rows, k), jnp.float32),
-        in_specs=[VMEM] * 4,
-        out_specs=VMEM,
+        out_shape=(out, out),
+        in_specs=[pl.BlockSpec(memory_space=pl.ANY)] * 4,
+        out_specs=(VMEM, VMEM),
         scratch_shapes=[
+            pltpu.VMEM(b.shape, jnp.float32),
+            pltpu.VMEM(a.shape, jnp.float32),
+            pltpu.VMEM(u.shape, jnp.float32),
+            pltpu.VMEM(v.shape, jnp.float32),
             pltpu.VMEM((bits + 1, 2 * rows, k), jnp.float32),
             pltpu.VMEM((bits, 2 * rows, k), jnp.float32),
-            pltpu.SemaphoreType.DMA((bits, 2)),
-            pltpu.SemaphoreType.DMA((bits, 2)),
+            pltpu.SemaphoreType.DMA((4,)),
+            pltpu.SemaphoreType.DMA((2, bits, 2)),
+            pltpu.SemaphoreType.DMA((2, bits, 2)),
         ],
         compiler_params=pltpu.CompilerParams(collective_id=0, has_side_effects=True),
     )(b, a, u, v)
@@ -115,7 +151,7 @@
     tenant = lax.axis_index("tenant")
     core = lax.rem(tenant, 2)
     place = tenant // 2
-    nch = other.shape[0]
+    nch = up.shape[0]
     lower = (place < chain // 2).astype(jnp.int32)
     toward = 2 * lower - 1
     mate = {"tenant": tenant + 1 - 2 * core}
@@ -136,7 +172,8 @@
 
     rows, width = f_ref.shape
     half = width // 2
-    tile = other.shape[1]
+    tile = up.shape[1]
+    block_rows = other.shape[1]
     weight = mm(x_ref[...], x_ref[...], 1, 1)
     same = lax.broadcasted_iota(jnp.int32, weight.shape, 0) // rank == lax.broadcasted_iota(
         jnp.int32, weight.shape, 1) // rank
@@ -146,11 +183,14 @@
     def rows_of(side, ch):
         return pl.ds(pl.multiple_of(side * half + ch * tile, tile), tile)
 
-    def term(side, ch):
-        return mm3(f_ref[:, rows_of(side, ch)], coeff[...], 0, 0)
-
-    def pair_copy(ch):
-        return remote(other.at[ch], pair.at[ch], pair_send.at[ch], pair_recv.at[ch], mate)
+    def block_of(side, at):
+        return pl.ds(pl.multiple_of(side * half + at * block_rows, block_rows), block_rows)
+
+    def term(side, at):
+        return mm3(f_ref[:, block_of(side, at)], coeff[...], 0, 0)
+
+    def pair_copy(at):
+        return remote(other.at[at], pair.at[at], pair_send.at[at], pair_recv.at[at], mate)
 
     def in_copy(ch, slot):
         return remote(up.at[ch], got.at[slot, ch], in_send.at[ch], recv.at[slot, ch], inner)
@@ -159,9 +199,9 @@
         mine = m_ref.at[rows_of(core, ch)]
         return remote(mine, got.at[1, ch], out_send.at[ch], recv.at[1, ch], outer)
 
-    def fin_copy(side, ch):
-        part = m_ref.at[rows_of(side, ch)]
-        return remote(part, part, fin_send.at[ch], fin_recv.at[ch], mate)
+    def fin_copy(side, at):
+        part = m_ref.at[block_of(side, at)]
+        return remote(part, part, fin_send.at[at], fin_recv.at[at], mate)
 
     acc[0] = jnp.zeros_like(acc[0])
 
@@ -170,12 +210,18 @@
         pair_copy(ch).start()
         return 0
 
-    lax.fori_loop(0, nch, first, 0)
+    lax.fori_loop(0, nch // 2, first, 0)
 
     def gather_up(ch):
-        up[ch] = term(core, ch)
-        pair_copy(ch).wait_recv()
-        up[ch] += pair[ch]
+        at = ch // 2
+
+        @pl.when(lax.rem(ch, 2) == 0)
+        def _():
+            whole = term(core, at)
+            pair_copy(at).wait_recv()
+            whole += pair[at]
+            up[ch] = whole[:tile]
+            up[ch + 1] = whole[tile:]
 
         @pl.when(jnp.logical_not(is_end))
         def _():
@@ -187,12 +233,13 @@
     k = m_ref.shape[1]
     part = pl.ds(pl.multiple_of(core * (k // 2), k // 2), k // 2)
 
-    def accumulate(ch):
-        fin_copy(1 - core, ch).wait_recv()
+    def accumulate(at):
+        fin_copy(1 - core, at).wait_recv()
         for side in range(2):
-            block = m_ref[rows_of(side, ch), :]
-            acc[0, :rows, :] += mm3(f_ref[:, rows_of(side, ch)], block, 1, 0)
-            acc[0, rows:, :] += mm(m_ref[rows_of(side, ch), part], block, 0, 0)
+            here = block_of(side, at)
+            block = m_ref[here, :]
+            acc[0, :rows, :] += mm3(f_ref[:, here], block, 1, 0)
+            acc[0, rows:, :] += mm(m_ref[here, part], block, 0, 0)
 
     def settle(ch):
         in_copy(ch, 1).wait_recv()
@@ -209,13 +256,15 @@
         def _():
             out_copy(ch).start()
 
-        fin_copy(core, ch).start()
-
-        @pl.when(ch > 0)
-        def _():
-            accumulate(ch - 1)
-
-    lag = 1 + 4 * dist
+        @pl.when(lax.rem(ch, 2) == 1)
+        def _():
+            fin_copy(core, ch // 2).start()
+
+        @pl.when(jnp.logical_and(lax.rem(ch, 2) == 0, ch > 0))
+        def _():
+            accumulate(ch // 2 - 1)
+
+    lag = 2 + 5 * dist
 
     def step(i, _):
         @pl.when(i < nch)
@@ -228,8 +277,8 @@
 
         return 0
 
-    lax.fori_loop(0, nch + 1 + 4 * (chain // 2 - 1), step, 0)
-    accumulate(nch - 1)
+    lax.fori_loop(0, nch + 2 + 5 * (chain // 2 - 1), step, 0)
+    accumulate(nch // 2 - 1)
     row_sum(bits, acc, rgot, row_send, row_recv)
     s_ref[:rows, :] = acc[bits, :rows, :]
 
@@ -241,9 +290,12 @@
     gram_copy(core).start()
 
     def drain(ch, _):
-        pair_copy(ch).wait_send()
         in_copy(ch, mid).wait_send()
-        fin_copy(core, ch).wait_send()
+
+        @pl.when(ch < nch // 2)
+        def _():
+            pair_copy(ch).wait_send()
+            fin_copy(core, ch).wait_send()
 
         @pl.when(jnp.logical_not(is_end))
         def _():
@@ -259,7 +311,8 @@
 def refresh(bits, chain, rank, f, x, y):
     rows, width = f.shape
     k = x.shape[1]
-    tile = min(LANES, width // 2)
+    wide = min(LANES, width // 2)
+    tile = wide // 2
     nch = width // 2 // tile
     f32 = jnp.float32
     dma = pltpu.SemaphoreType.DMA
@@ -269,15 +322,16 @@
         in_specs=[VMEM] * 3,
         out_specs=(VMEM, VMEM),
         scratch_shapes=[
-            pltpu.VMEM((nch, tile, k), f32),
-            pltpu.VMEM((nch, tile, k), f32),
+            pltpu.VMEM((nch // 2, wide, k), f32),
+            pltpu.VMEM((nch // 2, wide, k), f32),
             pltpu.VMEM((nch, tile, k), f32),
             pltpu.VMEM((2, nch, tile, k), f32),
             pltpu.VMEM((bits + 1, rows + k // 2, k), f32),
             pltpu.VMEM((bits, rows + k // 2, k), f32),
             pltpu.VMEM((rows, k), f32),
-            dma((nch,)), dma((nch,)), dma((nch,)), dma((2, nch)), dma((nch,)), dma((nch,)), dma((nch,)),
-            dma((bits, 2)), dma((bits, 2)), dma(()), dma(()),
+            dma((nch // 2,)), dma((nch // 2,)), dma((nch,)), dma((2, nch)), dma((nch,)), dma((nch // 2,)),
+            dma((nch // 2,)),
+            dma((1, bits, 2)), dma((1, bits, 2)), dma(()), dma(()),
         ],
         compiler_params=pltpu.CompilerParams(collective_id=1, has_side_effects=True),
     )(f, x, y)
@@ -362,8 +416,7 @@
     chain = mesh_shape["tenant"] // 2
     b = b_factors.reshape(rows, width)
     a = a_factors.reshape(rows, width)
-    both = start(bits, b, a, u_start, v_start)
-    left, right = both[:rows], both[rows:]
+    left, right = start(bits, b, a, u_start, v_start)
     basis_u, sums = refresh(bits, chain, rank, b, right, left)
     inv_u, left = factor(sums)
     basis_v, sums = refresh(bits, chain, rank, a, left, right)

time: 157 us -> 152 us (0.968)
  Pallas kernels: 147 us -> 143 us
  local copies, waits for them, and re-layouts: 1.68 us -> 0 us
    pallas_call x2, Pallas kernels: 107 us -> 105 us  [refresh(): pl.pallas_call(functools.partial(refresh_kernel, bits, chain, rank), out_...]
    slice x1 -> x0, local copies, waits for them, and re-layouts: 1.68 us -> none  [local(): left, right = (both[:rows], both[rows:])]
    pallas_call x1, Pallas kernels: 16.4 us -> 14.8 us  [start(): pl.pallas_call(functools.partial(start_kernel, bits), out_shape=(out, out...]
where the time goes in v3:
time: 152 us
  Pallas kernels  143 us (94%)
  matrix products  7.89 us (5%)
    pallas_call x2, Pallas kernels, refresh(): pl.pallas_call(functools.partial(refresh_kernel, bits, chain, rank), out_...  105 us
    pallas_call x2, Pallas kernels, factor(): pl.pallas_call(factor_kernel, out_shape=(jax.ShapeDtypeStruct((k, k), jnp...  23.6 us
    pallas_call x1, Pallas kernels, start(): pl.pallas_call(functools.partial(start_kernel, bits), out_shape=(out, out...  14.8 us
    dot_general x2, matrix products, finish(): lax.dot_general(basis, inv, (((1,), (1,)), ((), ())), precision=lax.Preci...  7.89 us

profile of v3, /device:TPU:0, one launch (start us, length us, event | category | flops | bytes accessed | tf_op | source)
XLA Modules:
  0.0 151.5 jit_solution(5294195937236536029)
XLA Ops:
  0.6 14.8 %shard_map.75 = (f32[128,256]{1,0:T(8,128)}, f32[128,256]{1,0:T(8,128)}) custom-call(f32[128,2048]{1,0:T(8,128)} %bitcast.6, f32[128,2048]{1,0:T(8,128)} %bitcast.8, f32[2048,256]{1,0:T(8,128)} %u_hbm.1, f32[2048,256]{1,0:T(8,128)} %v_hbm.1), custom_call_target="tpu_custom_call" | custom-call | tf_op jit(solution)/shard_map/pallas_call | solution.py:129
  15.4 52.3 %shard_map.76 = (f32[2048,256]{1,0:T(8,128)}, f32[384,256]{1,0:T(8,128)}) custom-call(f32[128,2048]{1,0:T(8,128)} %bitcast.7, f32[128,256]{1,0:T(8,128)} %get-tuple-element.14.x_ref.y_ref, f32[128,256]{1,0:T(8,128)} %get-tuple-element.15.y_ref), custom_call_target="tpu_custom_call" | custom-call | tf_op jit(solution)/shard_map/pallas_call | solution.py:319
  67.7 11.8 %shard_map.77 = (f32[256,256]{1,0:T(8,128)}, f32[128,256]{1,0:T(8,128)}) custom-call(f32[384,256]{1,0:T(8,128)} %get-tuple-element.17.s_ref), custom_call_target="tpu_custom_call" | custom-call | tf_op jit(solution)/shard_map/pallas_call | solution.py:398
  79.5 3.9 %fusion.2 = f32[2048,256]{1,0:T(8,128)} fusion(f32[2048,256]{1,0:T(8,128)} %get-tuple-element.16, f32[256,256]{1,0:T(8,128)} %get-tuple-element.18), kind=kOutput, calls=%fused_computation.2 | convolution fusion | flops 805371904 | bytes 4456448 | tf_op jit(solution)/shard_map/dot_general | solution.py:408
  83.4 52.3 %shard_map.78 = (f32[2048,256]{1,0:T(8,128)}, f32[384,256]{1,0:T(8,128)}) custom-call(f32[128,2048]{1,0:T(8,128)} %bitcast.9, f32[128,256]{1,0:T(8,128)} %get-tuple-element.19.x_ref, f32[128,256]{1,0:T(8,128)} %get-tuple-element.14.x_ref.y_ref), custom_call_target="tpu_custom_call" | custom-call | tf_op jit(solution)/shard_map/pallas_call | solution.py:319
  135.8 11.8 %shard_map.79 = (f32[256,256]{1,0:T(8,128)}, f32[128,256]{1,0:T(8,128)}) custom-call(f32[384,256]{1,0:T(8,128)} %get-tuple-element.21.s_ref), custom_call_target="tpu_custom_call" | custom-call | tf_op jit(solution)/shard_map/pallas_call | solution.py:398
  147.6 3.9 %fusion = f32[2048,256]{1,0:T(8,128)} fusion(f32[2048,256]{1,0:T(8,128)} %get-tuple-element.20, f32[256,256]{1,0:T(8,128)} %get-tuple-element.22), kind=kOutput, calls=%fused_computation | convolution fusion | flops 805371904 | bytes 4456448 | tf_op jit(solution)/shard_map/dot_general | solution.py:408

commit v4 on v3

--- a/solution.py
+++ b/solution.py
@@ -11,8 +11,10 @@
 HIGH = lax.Precision.HIGHEST
 MESH = pl.DeviceIdType.MESH
 VMEM = pl.BlockSpec(memory_space=pltpu.VMEM)
+ANY = pl.BlockSpec(memory_space=pl.ANY)
 LANES = 128
 BLK = 64
+OUT = 4
 
 
 def mm(x, y, cx, cy):
@@ -146,8 +148,10 @@
     )(b, a, u, v)
 
 
-def refresh_kernel(bits, chain, rank, f_ref, x_ref, y_ref, m_ref, s_ref, other, pair, up, got, acc, rgot, coeff,
+def refresh_kernel(bits, chain, rank, f_hbm, x_ref, y_ref, m_hbm, s_ref, f_ref, m_ref, load, store, other, pair, up, got, acc, rgot, coeff,
                    pair_send, pair_recv, in_send, recv, out_send, fin_send, fin_recv, row_send, row_recv, gram_send, gram_recv):
+    fetch = pltpu.make_async_copy(f_hbm, f_ref, load)
+    fetch.start()
     tenant = lax.axis_index("tenant")
     core = lax.rem(tenant, 2)
     place = tenant // 2
@@ -210,6 +214,7 @@
         pair_copy(ch).start()
         return 0
 
+    fetch.wait()
     lax.fori_loop(0, nch // 2, first, 0)
 
     def gather_up(ch):
@@ -233,10 +238,15 @@
     k = m_ref.shape[1]
     part = pl.ds(pl.multiple_of(core * (k // 2), k // 2), k // 2)
 
+    def keep(side, at):
+        here = block_of(side, at)
+        return pltpu.make_async_copy(m_ref.at[here], m_hbm.at[here], store.at[side, at])
+
     def accumulate(at):
         fin_copy(1 - core, at).wait_recv()
         for side in range(2):
             here = block_of(side, at)
+            keep(side, at).start()
             block = m_ref[here, :]
             acc[0, :rows, :] += mm3(f_ref[:, here], block, 1, 0)
             acc[0, rows:, :] += mm(m_ref[here, part], block, 0, 0)
@@ -296,6 +306,8 @@
         def _():
             pair_copy(ch).wait_send()
             fin_copy(core, ch).wait_send()
+            for side in range(2):
+                keep(side, ch).wait()
 
         @pl.when(jnp.logical_not(is_end))
         def _():
@@ -319,9 +331,12 @@
     return pl.pallas_call(
         functools.partial(refresh_kernel, bits, chain, rank),
         out_shape=(jax.ShapeDtypeStruct((width, k), f32), jax.ShapeDtypeStruct((rows + k, k), f32)),
-        in_specs=[VMEM] * 3,
-        out_specs=(VMEM, VMEM),
+        in_specs=[ANY, VMEM, VMEM],
+        out_specs=(ANY, VMEM),
         scratch_shapes=[
+            pltpu.VMEM((rows, width), f32),
+            pltpu.VMEM((width, k), f32),
+            dma(()), dma((2, nch // 2)),
             pltpu.VMEM((nch // 2, wide, k), f32),
             pltpu.VMEM((nch // 2, wide, k), f32),
             pltpu.VMEM((nch, tile, k), f32),
@@ -375,8 +390,10 @@
     return full[:, n:] * lax.rsqrt(diag)
 
 
-def factor_kernel(s_ref, inv_ref, left_ref, tab):
-    k = inv_ref.shape[0]
+def factor_kernel(scale, s_ref, m_hbm, out_hbm, left_ref, tab, m_ref, out_ref, load, store):
+    fetch = pltpu.make_async_copy(m_hbm, m_ref, load)
+    fetch.start()
+    k = s_ref.shape[1]
     rows = left_ref.shape[0]
     tab[:, :k] = s_ref[rows:, :]
     tab[:, k:] = (lax.broadcasted_iota(jnp.int32, (k, k), 0) == lax.broadcasted_iota(
@@ -388,24 +405,36 @@
         tab[at:end, :] = done
         if end < k:
             tab[end:, :] -= mm(done[:, end:k], done, 0, 0)
-    inv_ref[...] = tab[:, k:]
     left_ref[...] = mm(s_ref[:rows, :], tab[:, k:], 1, 1)
-
-
-def factor(s):
+    scaled = tab[:, k:] * scale
+    fetch.wait()
+    size = m_ref.shape[0] // OUT
+    copies = []
+    for i in range(OUT):
+        here = pl.ds(i * size, size)
+        out_ref[here, :] = mm3(m_ref[here, :], scaled, 1, 1)
+        copies.append(pltpu.make_async_copy(out_ref.at[here], out_hbm.at[here], store.at[i]))
+        copies[-1].start()
+    for copy in copies:
+        copy.wait()
+
+
+def factor(scale, s, m):
     k = s.shape[1]
     rows = s.shape[0] - k
     return pl.pallas_call(
-        factor_kernel,
-        out_shape=(jax.ShapeDtypeStruct((k, k), jnp.float32), jax.ShapeDtypeStruct((rows, k), jnp.float32)),
-        in_specs=[VMEM],
-        out_specs=(VMEM, VMEM),
-        scratch_shapes=[pltpu.VMEM((k, 2 * k), jnp.float32)],
-    )(s)
-
-
-def finish(basis, inv):
-    return lax.dot_general(basis, inv, (((1,), (1,)), ((), ())), precision=lax.Precision.HIGH)
+        functools.partial(factor_kernel, scale),
+        out_shape=(jax.ShapeDtypeStruct(m.shape, jnp.float32), jax.ShapeDtypeStruct((rows, k), jnp.float32)),
+        in_specs=[VMEM, ANY],
+        out_specs=(ANY, VMEM),
+        scratch_shapes=[
+            pltpu.VMEM((k, 2 * k), jnp.float32),
+            pltpu.VMEM(m.shape, jnp.float32),
+            pltpu.VMEM(m.shape, jnp.float32),
+            pltpu.SemaphoreType.DMA(()),
+            pltpu.SemaphoreType.DMA((OUT,)),
+        ],
+    )(s, m)
 
 
 def local(mesh_shape, b_factors, a_factors, u_start, v_start):
@@ -417,13 +446,11 @@
     b = b_factors.reshape(rows, width)
     a = a_factors.reshape(rows, width)
     left, right = start(bits, b, a, u_start, v_start)
+    scale = math.sqrt(width * mesh_shape["row"])
     basis_u, sums = refresh(bits, chain, rank, b, right, left)
-    inv_u, left = factor(sums)
+    u, left = factor(scale, sums, basis_u)
     basis_v, sums = refresh(bits, chain, rank, a, left, right)
-    inv_v, right = factor(sums)
-    scale = math.sqrt(width * mesh_shape["row"])
-    u = finish(basis_u, inv_u * scale)
-    v = finish(basis_v, inv_v * scale)
+    v, right = factor(scale, sums, basis_v)
     return u, v, left.reshape(nt, rank, k), right.reshape(nt, rank, k)
 
 

time: 152 us -> 149 us (0.980)
  matrix products: 7.89 us -> 0 us
  Pallas kernels: 143 us -> 148 us
    dot_general x2 -> x0, matrix products: 7.89 us -> none  [finish(): lax.dot_general(basis, inv, (((1,), (1,)), ((), ())), precision=lax.Preci...]
    pallas_call x2, Pallas kernels: 23.6 us -> 29.7 us  [factor(): pl.pallas_call(functools.partial(factor_kernel, scale), out_shape=(jax.Sh...]
where the time goes in v4:
time: 149 us; the launch traced here: 148 us
  Pallas kernels  148 us (99%)
    pallas_call x2, Pallas kernels, refresh(): pl.pallas_call(functools.partial(refresh_kernel, bits, chain, rank), out_...  103 us
    pallas_call x2, Pallas kernels, factor(): pl.pallas_call(functools.partial(factor_kernel, scale), out_shape=(jax.Sh...  29.7 us
    pallas_call x1, Pallas kernels, start(): pl.pallas_call(functools.partial(start_kernel, bits), out_shape=(out, out...  14.8 us

profile of v4, /device:TPU:0, one launch (start us, length us, event | category | flops | bytes accessed | tf_op | source)
XLA Modules:
  0.0 148.5 jit_solution(923738169554354327)
XLA Ops:
  0.6 14.8 %shard_map.75 = (f32[128,256]{1,0:T(8,128)}, f32[128,256]{1,0:T(8,128)}) custom-call(f32[128,2048]{1,0:T(8,128)} %bitcast.4, f32[128,2048]{1,0:T(8,128)} %bitcast.6, f32[2048,256]{1,0:T(8,128)} %u_hbm.1, f32[2048,256]{1,0:T(8,128)} %v_hbm.1), custom_call_target="tpu_custom_call" | custom-call | tf_op jit(solution)/shard_map/pallas_call | solution.py:131
  15.4 52.2 %shard_map.76 = (f32[2048,256]{1,0:T(8,128)}, f32[384,256]{1,0:T(8,128)}) custom-call(f32[128,2048]{1,0:T(8,128)} %bitcast.5, f32[128,256]{1,0:T(8,128)} %get-tuple-element.14.x_ref.y_ref, f32[128,256]{1,0:T(8,128)} %get-tuple-element.15.y_ref), custom_call_target="tpu_custom_call" | custom-call | tf_op jit(solution)/shard_map/pallas_call | solution.py:331
  67.6 14.9 %shard_map.77 = (f32[2048,256]{1,0:T(8,128)}, f32[128,256]{1,0:T(8,128)}) custom-call(f32[384,256]{1,0:T(8,128)} %get-tuple-element.16.s_ref, f32[2048,256]{1,0:T(8,128)} %get-tuple-element.17.m_hbm), custom_call_target="tpu_custom_call" | custom-call | tf_op jit(solution)/shard_map/pallas_call | solution.py:425
  82.5 51.0 %shard_map.78 = (f32[2048,256]{1,0:T(8,128)}, f32[384,256]{1,0:T(8,128)}) custom-call(f32[128,2048]{1,0:T(8,128)} %bitcast.7, f32[128,256]{1,0:T(8,128)} %get-tuple-element.19.x_ref, f32[128,256]{1,0:T(8,128)} %get-tuple-element.14.x_ref.y_ref), custom_call_target="tpu_custom_call" | custom-call | tf_op jit(solution)/shard_map/pallas_call | solution.py:331
  133.4 14.9 %shard_map.79 = (f32[2048,256]{1,0:T(8,128)}, f32[128,256]{1,0:T(8,128)}) custom-call(f32[384,256]{1,0:T(8,128)} %get-tuple-element.20.s_ref, f32[2048,256]{1,0:T(8,128)} %get-tuple-element.21.m_hbm), custom_call_target="tpu_custom_call" | custom-call | tf_op jit(solution)/shard_map/pallas_call | solution.py:425
